TPU v7x, 1024 devices: a whole 4x4x32 slice. The times are simulated.
1024 devices in a mesh: ctx: 128 (over x, z), fsdp: 8 (over y, core).
Axes of the slice: x: 4, y: 4, z: 32, core: 2. Of those that a mesh axis runs over, the one named last changes fastest.
Arguments:
- query_rows: bfloat16 [16384, 4096], P('ctx', 'fsdp'), may hold values from -6 to 6
- key_rows: bfloat16 [16384, 4096], P('ctx', 'fsdp'), may hold values from -6 to 6
- value_rows: bfloat16 [16384, 4096], P('ctx', 'fsdp'), may hold values from -6 to 6
- filters: float32 [256, 128], P('fsdp'), may hold values from -0.5 to 0.5
- out_weight: bfloat16 [4096, 4096], P('ctx', 'fsdp'), may hold values from -0.09375 to 0.09375
- out_grad: bfloat16 [16384, 4096], P('ctx', 'fsdp'), may hold values from -6 to 6
Outputs:
- mixed_out: bfloat16 [16384, 4096], P('ctx', 'fsdp')
- query_grad: bfloat16 [16384, 4096], P('ctx', 'fsdp')
- key_grad: bfloat16 [16384, 4096], P('ctx', 'fsdp')
- value_grad: bfloat16 [16384, 4096], P('ctx', 'fsdp')
All inputs are finite; a program needn't handle non-finite values.
Results may differ from a plain program's by a relative error of at most 0.022.
Values may be sent and summed in bfloat16 or wider, within the bound.
A program may use at most 64 MiB of HBM per device.

v0:
```python
import jax
import jax.numpy as jnp
from jax import lax
from jax.sharding import PartitionSpec as P


def passed_along(block, axis, distance):
    devices = range(lax.axis_size(axis))
    route = [(i - distance, i) for i in devices if i - distance in devices]
    return lax.ppermute(block, axis, route)


def split_band(filters, lag_table):
    tap_count = filters.shape[1]
    inside = (lag_table >= 0) & (lag_table < tap_count)
    picked = jnp.take(filters, jnp.clip(lag_table, 0, tap_count - 1), axis=1)
    band_table = jnp.where(inside[None, :, :], picked, 0.0)
    band_high = band_table.astype(jnp.bfloat16)
    band_low = (band_table - band_high.astype(jnp.float32)).astype(jnp.bfloat16)
    return (band_high, band_low)


def apply_band(band_high, band_low, extended, tok_rows):
    group_count = band_high.shape[0]
    channels = extended.shape[1]
    shaped = extended.reshape(extended.shape[0], group_count, channels // group_count)
    result = jnp.einsum("gts,sgc->tgc", band_high, shaped, preferred_element_type=jnp.float32)
    result = result + jnp.einsum(
        "gts,sgc->tgc", band_low, shaped, preferred_element_type=jnp.float32
    )
    return result.reshape(tok_rows, channels)


def on_device(query_rows, key_rows, value_rows, filters, out_weight, out_grad):
    tok_rows = query_rows.shape[0]
    rim_rows = filters.shape[1] - 1
    query_wide = query_rows.astype(jnp.float32)
    key_wide = key_rows.astype(jnp.float32)
    value_wide = value_rows.astype(jnp.float32)
    product = (key_wide * value_wide).astype(jnp.bfloat16)
    previous = passed_along(product[tok_rows - rim_rows :], "ctx", 1)
    extended = jnp.concatenate([previous, product], axis=0)
    row_index = lax.broadcasted_iota(jnp.int32, (tok_rows, tok_rows + rim_rows), 0)
    col_index = lax.broadcasted_iota(jnp.int32, (tok_rows, tok_rows + rim_rows), 1)
    band_high, band_low = split_band(filters, row_index + rim_rows - col_index)
    conv = apply_band(band_high, band_low, extended, tok_rows)
    gated = (query_wide * conv).astype(jnp.bfloat16)
    panel_cols = lax.all_gather(out_weight, "ctx", axis=0, tiled=True)
    summed = jnp.dot(
        lax.all_gather(gated, "fsdp", axis=1, tiled=True),
        panel_cols,
        preferred_element_type=jnp.float32,
    )
    mixed_out = summed.astype(jnp.bfloat16)
    partials = lax.dot_general(
        out_grad, panel_cols, (((1,), (1,)), ((), ())), preferred_element_type=jnp.float32
    )
    gate_grad = lax.psum_scatter(
        partials.astype(jnp.bfloat16), "fsdp", scatter_dimension=1, tiled=True
    ).astype(jnp.float32)
    conv_grad = (gate_grad * query_wide).astype(jnp.bfloat16)
    query_grad = (gate_grad * conv).astype(jnp.bfloat16)
    following = passed_along(conv_grad[:rim_rows], "ctx", -1)
    extended_grad = jnp.concatenate([conv_grad, following], axis=0)
    product_grad = apply_band(
        band_high[:, ::-1, ::-1], band_low[:, ::-1, ::-1], extended_grad, tok_rows
    )
    key_grad = (product_grad * value_wide).astype(jnp.bfloat16)
    value_grad = (product_grad * key_wide).astype(jnp.bfloat16)
    return (mixed_out, query_grad, key_grad, value_grad)


def solution(mesh):
    return jax.shard_map(
        on_device,
        mesh=mesh,
        in_specs=(
            P("ctx", "fsdp"),
            P("ctx", "fsdp"),
            P("ctx", "fsdp"),
            P("fsdp", None),
            P("ctx", "fsdp"),
            P("ctx", "fsdp"),
        ),
        out_specs=(P("ctx", "fsdp"), P("ctx", "fsdp"), P("ctx", "fsdp"), P("ctx", "fsdp")),
        check_vma=False,
    )
```

profile of v0, /device:TPU:1, one launch (start us, length us, event | category | flops | bytes accessed | tf_op | source)
XLA Modules:
  0.0 503.9 jit_solution(10463339483110685715)
XLA Ops:
  7.2 0.7 all-gather.5.cloned.1.call-update
  8.0 267.1 %all-gather.5.cloned.1.call-done = bf16[4096,512]{1,0:T(8,128)(2,1)} async-done(((bf16[32,512]{1,0:T(8,128)(2,1)}), bf16[4096,512]{1,0:T(8,128)(2,1)}) %all-gather.5.cloned.1.call-update) | async-done | bytes 4194320 | tf_op jit(solution)/shard_map/all_gather | solution.py:48
  275.1 4.7 convolution_convert_fusion
  280.0 0.3 reshape.94
  280.5 60.7 %gather_fusion = f32[32640,32]{1,0:T(8,128)} fusion(f32[32,128]{0,1:T(8,128)S(1)} %copy.20, s32[32768]{0:T(1024)S(1)} %pad_clamp_fusion), kind=kCustom, calls=%fused_computation | custom fusion | bytes 8486400 | tf_op jit(solution)/shard_map/jit(_take)/gather | solution.py:16
  341.1 11.6 %copy.21 = f32[32640,32]{0,1:T(8,128)} copy(f32[32640,32]{1,0:T(8,128)} %gather_fusion) | data formatting | bytes 8355840 | tf_op jit(solution)/shard_map/jit(_take)/gather | solution.py:16
  352.7 9.4 %reshape.97 = f32[128,255,32]{1,0,2:T(8,128)} reshape(f32[32640,32]{0,1:T(8,128)} %copy.21) | data formatting | bytes 8355840 | tf_op jit(solution)/shard_map/jit(_take)/gather | solution.py:16
  362.1 0.2 fusion.11
  362.3 0.9 fusion.6
  363.3 1.3 collective-permute-start.1
  364.6 4.4 fusion
  368.9 32.0 %reverse = bf16[32,128,256]{2,1,0:T(8,128)(2,1)} reverse(bf16[32,128,256]{2,1,0:T(8,128)(2,1)} %bitcast.32), dimensions={1,2} | reverse | bytes 4194304
  400.9 22.6 %reverse.1 = bf16[32,128,256]{2,1,0:T(8,128)(2,1)} reverse(bf16[32,128,256]{2,1,0:T(8,128)(2,1)S(1)} %bitcast.31), dimensions={1,2} | reverse | bytes 4194304
  423.7 2.5 fusion.14
  426.2 0.8 convolution_add_fusion
  427.2 0.8 fusion.2
  428.0 4.0 collective-permute-start
  432.0 1.9 collective-permute-done
  434.1 2.2 fusion.16
  436.3 0.7 convolution_add_fusion.1
  437.0 0.1 copy.22
  437.3 0.7 fusion.5
  438.0 55.4 %all-gather.3.cloned.1.call-done = bf16[128,4096]{1,0:T(8,128)(2,1)} async-done(((bf16[128,512]{1,0:T(8,128)(2,1)}), bf16[128,4096]{1,0:T(8,128)(2,1)}) %all-gather.3.cloned.1.call-update) | async-done | bytes 1048592 | tf_op jit(solution)/shard_map/all_gather | solution.py:50
  493.5 3.9 convolution_convert_fusion.1
  (31 shorter events, 1.1 us)
Async XLA Ops:
  7.2 267.9 %copy-start = (bf16[128,512]{1,0:T(8,128)(2,1)S(1)}, bf16[128,512]{1,0:T(8,128)(2,1)}, u32[]{:S(2)}) copy-start(bf16[128,512]{1,0:T(8,128)(2,1)} %param.11) | copy-start | bytes 393220
  7.2 267.9 %all-gather.5.cloned.1.call-start = ((), (), s32[]{:S(2)}) async-start(), calls=%async_computation.2 | async-start | bytes 4227072 | tf_op jit(solution)/shard_map/all_gather | solution.py:48
  7.9 272.4 %copy-start.6 = (f32[32,128]{1,0:T(8,128)S(1)}, f32[32,128]{1,0:T(8,128)}, u32[]{:S(2)}) copy-start(f32[32,128]{1,0:T(8,128)} %param.9) | copy-start | bytes 49156
  7.9 354.4 %reduce-scatter.2.cloned.1.call-start = ((), (), s32[]{:S(2)}) async-start(), calls=%async_computation.3 | async-start | bytes 1179648 | tf_op jit(solution)/shard_map/reduce_scatter | solution.py:58
  279.8 213.6 %all-gather.3.cloned.1.call-start = ((), (), s32[]{:S(2)}) async-start(), calls=%async_computation.1 | async-start | bytes 1179648 | tf_op jit(solution)/shard_map/all_gather | solution.py:50
  352.7 9.6 %copy-start.2 = (bf16[128,512]{1,0:T(8,128)(2,1)S(1)}, bf16[128,512]{1,0:T(8,128)(2,1)}, u32[]{:S(2)}) copy-start(bf16[128,512]{1,0:T(8,128)(2,1)} %param.6) | copy-start | bytes 393220
  363.3 60.3 %collective-permute-start.1 = (bf16[127,512]{1,0:T(8,128)(2,1)S(1)}, bf16[127,512]{1,0:T(8,128)(2,1)S(1)}, u32[]{:S(2)}, u32[]{:S(2)}) collective-permute-start(bf16[127,512]{1,0:T(8,128)(2,1)S(1)} %bitcast.39), channel_id=1, source_target_pairs={{8,0},{16,8},{24,16},{32,24},{40,32},{48,40},{56,48},{64,56},{72,6... | collective-permute-start | bytes 390152 | tf_op jit(solution)/shard_map/ppermute | solution.py:10
  423.7 2.5 copy-start.1
  426.2 0.9 copy-start.4
  426.2 1.0 copy-start.5
  428.0 5.9 %collective-permute-start = (bf16[127,512]{1,0:T(8,128)(2,1)S(1)}, bf16[127,512]{1,0:T(8,128)(2,1)S(1)}, u32[]{:S(2)}, u32[]{:S(2)}) collective-permute-start(bf16[127,512]{1,0:T(8,128)(2,1)S(1)} %slice.10), channel_id=1, source_target_pairs={{0,8},{8,16},{16,24},{24,32},{32,40},{40,48},{48,56},{56,64},{64,7... | collective-permute-start | bytes 390152 | tf_op jit(solution)/shard_map/ppermute | solution.py:10
  436.3 0.9 copy-start.3
Sparse Core Ops, SparseCore 0:
  12.1 262.8 all-gather.4
  279.9 57.7 reduce-scatter.1
  438.2 55.2 all-gather.2
where the time goes:
time: 508 us; the launch traced here: 504 us
  waiting for transfers between devices  325 us (64%)
  local copies, waits for them, and re-layouts  137 us (27%)
  matrix products  14.8 us (3%)
  between operations  13.9 us (3%)
  other arithmetic  7.16 us (1%)
  starting transfers between devices  5.4 us (1%)
    all_gather x1, waiting for transfers between devices, on_device(): panel_cols = lax.all_gather(out_weight, 'ctx', axis=0, tiled=True)  267 us
    gather x3, local copies, waits for them, and re-layouts, split_band(): picked = jnp.take(filters, jnp.clip(lag_table, 0, tap_count - 1), axis=1)  81.7 us
    all_gather x1, waiting for transfers between devices, on_device(): lax.all_gather(gated, 'fsdp', axis=1, tiled=True)  55.4 us
    unnamed x17, local copies, waits for them, and re-layouts  54.9 us
  transfers between devices with their start and end apart: 5, of which 3 were waited for; matrix products, arithmetic and copies ran while one was open for 28% of the time, Pallas kernels for 0%

commit v1 on v0

v1 whole, which is shorter than its diff:
```python
import functools

import jax
import jax.numpy as jnp
from jax import lax
from jax.experimental import pallas as pl
from jax.experimental.pallas import tpu as pltpu
from jax.sharding import PartitionSpec as P

MESH = pl.DeviceIdType.MESH
BF = jnp.bfloat16
F32 = jnp.float32
SUB = 128
X_CHIPS = 4
A_COLS = 384


def kernel(
    X, Z, NF,
    q_hbm, k_hbm, v_hbm, f_hbm, w_hbm, og_hbm,
    mix_o, qg_o, kg_o, vg_o,
    q, k, v, og, filt, w, ext, band_f, band_b, conv, gated, stage, recv, cg, nxt, pg,
    load_sem, own_sem, za_send, xa_send, zb_send, xb_send, za, xr, xrel, zb, xb,
    g_send, g_recv, r_send, r_recv, p_send, p_recv, c_send, c_recv,
):
    C = X * Z
    rows = w_hbm.shape[0]
    CA = A_COLS
    cols = w_hbm.shape[1]
    M = Z // 4
    NG = Z * rows // SUB
    LT = q_hbm.shape[1] // SUB
    tok = q_hbm.shape[0]
    ctx = lax.axis_index("ctx")
    f = lax.axis_index("fsdp")
    x, z = ctx // Z, ctx % Z

    def dev(xx, zz):
        return (((xx + X) % X) * Z + (zz + Z) % Z, f)

    def wrap(zz):
        return (zz + Z) % Z

    barrier = pltpu.get_barrier_semaphore()
    partners = [dev(x, z + 1), dev(x, z - 1), dev(x, z + 2), dev(x, z - 2)]
    partners += [dev(x + 1, z), dev(x - 1, z), dev(x + 2, z)]
    partners += [((ctx + 1) % C, f), ((ctx + C - 1) % C, f)]
    partners += [(ctx, (f + s) % NF) for s in range(1, NF)]
    for who in partners:
        pl.semaphore_signal(barrier, inc=1, device_id=who, device_id_type=MESH)

    loads = [(k_hbm, k), (v_hbm, v), (f_hbm, filt), (q_hbm, q), (og_hbm, og)]
    loads = [pltpu.make_async_copy(a, b, load_sem.at[i]) for i, (a, b) in enumerate(loads)]
    own = pltpu.make_async_copy(w_hbm, w.at[x, pl.ds(z * rows, rows), :], own_sem)
    own.start()
    for c in loads:
        c.start()
    pl.semaphore_wait(barrier, len(partners))

    def a_ref(xx, zz):
        return w.at[(xx + X) % X, pl.ds(pl.multiple_of(wrap(zz) * rows, rows), rows), pl.ds(0, CA)]

    def b_ref(zz):
        return w.at[:, pl.ds(pl.multiple_of(wrap(zz) * rows, rows), rows), pl.ds(CA, cols - CA)]

    def remote(src, dst, ssem, rsem, who):
        pltpu.make_async_remote_copy(
            src_ref=src, dst_ref=dst, send_sem=ssem, recv_sem=rsem, device_id=who, device_id_type=MESH
        ).start()

    def wait(ref, sem):
        pltpu.make_async_copy(ref, ref, sem).wait()

    def chain_a(d, o, dist, src=None):
        sgn = 1 - 2 * d
        ref = a_ref(x, z - sgn * o)
        remote(ref if src is None else src, ref, za_send, za.at[d, o + dist], dev(x, z + sgn * dist))

    def chain_b(d, o, dist):
        sgn = 1 - 2 * d
        ref = b_ref(z - sgn * o)
        remote(ref, ref, zb_send, zb.at[d, o + dist], dev(x, z + sgn * dist))

    def spread(zs, src=None):
        ref = a_ref(x, zs)
        for side in (0, 1):
            remote(ref if src is None else src, ref, xa_send, xr.at[side, wrap(zs)], dev(x + 1 - 2 * side, z))

    def relay(zs):
        p = wrap(zs) % 2
        ref = a_ref(x - 1 + 2 * p, zs)
        wait(ref, xr.at[p, wrap(zs)])
        remote(ref, ref, xa_send, xrel.at[wrap(zs)], dev(x + 1 - 2 * p, z))

    own_a = w_hbm.at[:, pl.ds(0, CA)]
    for d in (0, 1):
        chain_a(d, 0, 2, own_a)
    for d in (0, 1):
        chain_a(d, 0, 1, own_a)
    own_b = w_hbm.at[:, pl.ds(CA, cols - CA)]
    my_b = w.at[x, pl.ds(pl.multiple_of(z * rows, rows), rows), pl.ds(CA, cols - CA)]
    for i, s in enumerate((1, 3, 2)):
        remote(own_b, my_b, xb_send, xb.at[i], dev(x + s, z))
    spread(z, own_a)

    loads[0].wait()
    loads[1].wait()
    for j in range(LT):
        lanes = slice(j * SUB, (j + 1) * SUB)
        prod = k[:, lanes].astype(F32) * v[:, lanes].astype(F32)
        ext[j, tok:, :] = prod.astype(BF)

    @pl.when(ctx < C - 1)
    def _():
        remote(ext.at[:, pl.ds(tok, tok), :], ext.at[:, pl.ds(0, tok), :], p_send, p_recv, ((ctx + 1) % C, f))

    @pl.when(ctx == 0)
    def _():
        ext[:, 0:tok, :] = jnp.zeros((LT, tok, SUB), BF)

    own.wait()
    for i in range(3):
        wait(my_b, xb.at[i])
    for d in (0, 1):
        chain_b(d, 0, 2)
    for d in (0, 1):
        chain_b(d, 0, 1)

    def step(m):
        wait(a_ref(x, z - 2 * m), za.at[0, 2 * m])

        @pl.when(m < M)
        def _():
            chain_a(0, 2 * m, 2)
            wait(a_ref(x, z + 2 * m), za.at[1, 2 * m])

            @pl.when(m < M - 1)
            def _():
                chain_a(1, 2 * m, 2)

            chain_a(0, 2 * m, 1)
            chain_a(1, 2 * m, 1)

        wait(b_ref(z - 2 * m), zb.at[0, 2 * m])

        @pl.when(m < M)
        def _():
            chain_b(0, 2 * m, 2)
            wait(b_ref(z + 2 * m), zb.at[1, 2 * m])

            @pl.when(m < M - 1)
            def _():
                chain_b(1, 2 * m, 2)

            chain_b(0, 2 * m, 1)
            chain_b(1, 2 * m, 1)
            spread(z + 2 * m)

        spread(z - 2 * m)
        for d in (0, 1):
            sgn = 1 - 2 * d
            zs = z - sgn * (2 * m - 1)
            wait(a_ref(x, zs), za.at[d, 2 * m - 1])
            spread(zs)
            wait(b_ref(zs), zb.at[d, 2 * m - 1])

        @pl.when(m > 1)
        def _():
            for zs in (z - 2 * m + 2, z + 2 * m - 2, z - 2 * m + 3, z + 2 * m - 3):
                relay(zs)

        @pl.when(m == 1)
        def _():
            relay(z)

    zg = z * rows // SUB
    per = SUB // rows

    def dgate(group):
        for i in range(per):
            zs = group * per + i
            p = zs % 2
            wait(a_ref(x + 1 - 2 * p, zs), xr.at[1 - p, zs])
            wait(a_ref(x + 2, zs), xrel.at[zs])
        at = pl.ds(pl.multiple_of(group * SUB, SUB), SUB)
        for xx in range(X):
            part = lax.dot_general(
                og[...], w[xx, at, :], (((1,), (1,)), ((), ())), preferred_element_type=F32
            ).astype(BF)
            sub = xx * NG + group
            owner, lane = sub // LT, sub % LT

            @pl.when(owner == f)
            def _():
                recv[f, lane, :, :] = part

            @pl.when(owner != f)
            def _():
                stage[sub, :, :] = part
                remote(stage.at[sub], recv.at[f, lane], r_send, r_recv.at[f, lane], (ctx, owner))

    def mixed(lo, hi):
        def body(g, carry):
            at = pl.ds(pl.multiple_of(g * SUB, SUB), SUB)
            acc = pg[...]
            for xx in range(X):
                acc = acc + jnp.dot(gated[xx * NG + g], w[xx, at, :], preferred_element_type=F32)
            pg[...] = acc
            return carry

        lax.fori_loop(lo, hi, body, 0)

    def bands():
        loads[2].wait()
        taps = filt[...].astype(BF)
        i0 = lax.broadcasted_iota(jnp.int32, (SUB, 2 * SUB), 0)
        i1 = lax.broadcasted_iota(jnp.int32, (SUB, 2 * SUB), 1)
        flip = jnp.where(i0 + i1 == SUB, 1.0, 0.0).astype(BF)
        keep = jnp.where(i0 == i1, 1.0, 0.0).astype(BF)
        pg_f = jnp.dot(taps, flip, preferred_element_type=F32)
        pg_b = jnp.dot(taps, keep, preferred_element_type=F32)
        return pg_f, pg_b

    def build(base, band):
        for g in range(base.shape[0]):
            row = jnp.broadcast_to(base[g : g + 1, :], (SUB, 2 * SUB))
            band[g * SUB : (g + 1) * SUB, :] = pltpu.roll(row, 0, 1, stride=1, stride_axis=0).astype(BF)

    lane_group = lax.broadcasted_iota(jnp.int32, (tok, SUB), 1) // 16

    def apply(band, lo, hi, data, j):
        n = SUB // 16
        res = jnp.dot(band[j * n * SUB : (j + 1) * n * SUB, lo:hi], data, preferred_element_type=F32)
        out = res[0:SUB]
        for g in range(1, n):
            out = jnp.where(lane_group == g, res[g * SUB : (g + 1) * SUB], out)
        return out

    step(1)
    base_f, base_b = bands()
    build(base_f, band_f)
    step(2)

    @pl.when(ctx > 0)
    def _():
        wait(ext.at[:, pl.ds(0, tok), :], p_recv)

    loads[3].wait()
    for j in range(LT):
        cv = apply(band_f, 0, 2 * SUB, ext[j], j)
        conv[j, :, :] = cv
        gated[f * LT + j, :, :] = (q[:, j * SUB : (j + 1) * SUB].astype(F32) * cv).astype(BF)
    mine = gated.at[pl.ds(f * LT, LT)]
    for s in range(1, NF):
        remote(mine, mine, g_send, g_recv.at[f], (ctx, (f + s) % NF))
    build(base_b, band_b)
    loads[4].wait()

    def loop(kk, carry):
        step(2 * kk + 1)

        def groups(i, c):
            dgate((zg + (1 - 2 * i) * (kk - 1) + NG) % NG)
            return c

        lax.fori_loop(0, jnp.where(kk == 1, 1, 2), groups, 0)
        step(2 * kk + 2)
        return carry

    lax.fori_loop(1, M // 2, loop, 0)
    for zs in (z - 2 * M, z - 2 * M + 1, z + 2 * M - 1):
        relay(zs)

    def last_groups(i, c):
        dgate((zg + M // 2 - 1 + i) % NG)
        return c

    lax.fori_loop(0, 2 if M == 2 else 3, last_groups, 0)

    for s in range(1, NF):
        src = (f + s) % NF
        wait(gated.at[pl.ds(src * LT, LT)], g_recv.at[src])
    pg[...] = jnp.zeros_like(pg)
    mixed(0, NG // 2)

    for j in range(LT):
        total = recv[f, j, :, :].astype(F32)
        for s in range(1, NF):
            src = (f + s) % NF
            wait(recv.at[src, j], r_recv.at[src, j])
            total = total + recv[src, j, :, :].astype(F32)
        lanes = slice(j * SUB, (j + 1) * SUB)
        cg[j, :, :] = (total * q[:, lanes].astype(F32)).astype(BF)
        qg_o[:, lanes] = (total * conv[j, :, :]).astype(BF)

        @pl.when(ctx > 0)
        def _():
            remote(cg.at[j], nxt.at[j], c_send.at[j], c_recv.at[j], ((ctx + C - 1) % C, f))

    mixed(NG // 2, NG)
    mix_o[...] = pg[...].astype(BF)
    for j in range(LT):
        conv[j, :, :] = apply(band_b, 0, SUB, cg[j], j)

    @pl.when(ctx == C - 1)
    def _():
        nxt[...] = jnp.zeros_like(nxt)

    for j in range(LT):
        @pl.when(ctx < C - 1)
        def _():
            wait(nxt.at[j], c_recv.at[j])

        lanes = slice(j * SUB, (j + 1) * SUB)
        both = conv[j, :, :] + apply(band_b, SUB, 2 * SUB, nxt[j], j)
        kg_o[:, lanes] = (both * v[:, lanes].astype(F32)).astype(BF)
        vg_o[:, lanes] = (both * k[:, lanes].astype(F32)).astype(BF)

    wait(w.at[0, pl.ds(0, (Z - 1) * rows), pl.ds(0, CA)], za_send)
    wait(w.at[pl.ds(0, 3), :, pl.ds(0, CA)], xa_send)
    wait(w.at[:, pl.ds(0, (Z - 1) * rows), pl.ds(CA, cols - CA)], zb_send)
    wait(w.at[pl.ds(0, 3), pl.ds(0, rows), pl.ds(CA, cols - CA)], xb_send)
    wait(gated.at[pl.ds(0, (NF - 1) * LT)], g_send)
    wait(gated.at[pl.ds(0, (NF - 1) * LT)], r_send)

    @pl.when(ctx < C - 1)
    def _():
        wait(ext.at[:, pl.ds(0, tok), :], p_send)

    @pl.when(ctx > 0)
    def _():
        for j in range(LT):
            wait(cg.at[j], c_send.at[j])


def solution(mesh):
    NF = mesh.shape["fsdp"]
    X = X_CHIPS
    Z = mesh.shape["ctx"] // X

    def on_device(q, k, v, f, w, og):
        tok, ch = q.shape
        lt = ch // SUB
        subs = NF * lt
        rows, cols = w.shape
        dma = pltpu.SemaphoreType.DMA
        out = jax.ShapeDtypeStruct((tok, ch), BF)
        return pl.pallas_call(
            functools.partial(kernel, X, Z, NF),
            out_shape=(jax.ShapeDtypeStruct((tok, cols), BF), out, out, out),
            in_specs=[pl.BlockSpec(memory_space=pl.ANY)] * 6,
            out_specs=tuple([pl.BlockSpec(memory_space=pltpu.VMEM)] * 4),
            scratch_shapes=[
                pltpu.VMEM((tok, ch), BF),
                pltpu.VMEM((tok, ch), BF),
                pltpu.VMEM((tok, ch), BF),
                pltpu.VMEM((tok, cols), BF),
                pltpu.VMEM(f.shape, F32),
                pltpu.VMEM((X, Z * rows, cols), BF),
                pltpu.VMEM((lt, 2 * tok, SUB), BF),
                pltpu.VMEM((f.shape[0] * SUB, 2 * SUB), BF),
                pltpu.VMEM((f.shape[0] * SUB, 2 * SUB), BF),
                pltpu.VMEM((lt, tok, SUB), F32),
                pltpu.VMEM((subs, tok, SUB), BF),
                pltpu.VMEM((subs, tok, SUB), BF),
                pltpu.VMEM((NF, lt, tok, SUB), BF),
                pltpu.VMEM((lt, tok, SUB), BF),
                pltpu.VMEM((lt, tok, SUB), BF),
                pltpu.VMEM((tok, cols), F32),
                dma((5,)), dma, dma, dma, dma, dma,
                dma((2, Z // 2 + 1)), dma((2, Z)), dma((Z,)), dma((2, Z // 2 + 1)), dma((3,)),
                dma, dma((NF,)), dma, dma((NF, lt)), dma, dma, dma((lt,)), dma((lt,)),
            ],
            compiler_params=pltpu.CompilerParams(
                collective_id=0, has_side_effects=True, vmem_limit_bytes=48 * 1024 * 1024
            ),
        )(q, k, v, f, w, og)

    wide = P("ctx", "fsdp")
    return jax.shard_map(
        on_device,
        mesh=mesh,
        in_specs=(wide, wide, wide, P("fsdp", None), wide, wide),
        out_specs=(wide, wide, wide, wide),
        check_vma=False,
    )
```

time: 508 us -> 91.6 us (0.18)
  waiting for transfers between devices: 325 us -> 0 us
  local copies, waits for them, and re-layouts: 137 us -> 7.7 us
  Pallas kernels: 0 us -> 82.9 us
  matrix products: 14.8 us -> 0 us
  between operations: 13.9 us -> 0.66 us
  other arithmetic: 7.16 us -> 0 us
  starting transfers between devices: 5.4 us -> 0 us
    all_gather x2 -> x0, waiting for transfers between devices: 323 us -> none  [the longest x1 267 us: on_device(): panel_cols = lax.all_gather(out_weight, 'ctx', axis=0, tiled=True)]
    pallas_call x0 -> x1, Pallas kernels: none -> 82.9 us  [on_device(): pl.pallas_call(functools.partial(kernel, X, Z, NF), out_shape=(jax.ShapeD...]
    gather x3 -> x0, local copies, waits for them, and re-layouts: 81.7 us -> none  [split_band(): picked = jnp.take(filters, jnp.clip(lag_table, 0, tap_count - 1), axis=1)]
    unnamed x17 -> x16, local copies, waits for them, and re-layouts: 54.9 us -> 7.7 us
    dot_general x6 -> x0, matrix products: 14.8 us -> none  [the longest x1 4.74 us: on_device(): lax.dot_general(out_grad, panel_cols, (((1,), (1,)), ((), ())), preferred...]
    convert_element_type x4 -> x0, other arithmetic: 6.82 us -> none  [the longest x1 4.37 us: split_band(): band_low = (band_table - band_high.astype(jnp.float32)).astype(jnp.bfloat16)]
    ppermute x2 -> x0, starting transfers between devices: 5.29 us -> none  [passed_along(): return lax.ppermute(block, axis, route)]
  transfers between devices with their start and end apart: 5 -> 0, of which waited for: 3 -> 0; matrix products, arithmetic and copies ran while one was open for 28% -> 0% of each run, Pallas kernels for 0% -> 0%
where the time goes in v1:
time: 91.6 us; the launch traced here: 91.3 us
  Pallas kernels  82.9 us (91%)
  local copies, waits for them, and re-layouts  7.7 us (8%)
    pallas_call x1, Pallas kernels, on_device(): pl.pallas_call(functools.partial(kernel, X, Z, NF), out_shape=(jax.ShapeD...  82.9 us
    unnamed x16, local copies, waits for them, and re-layouts  7.7 us

profile of v1, /device:TPU:1, one launch (start us, length us, event | category | flops | bytes accessed | tf_op | source)
XLA Modules:
  0.0 91.3 jit_solution(13338720720700973967)
XLA Ops:
  0.6 0.0 copy-start
  0.6 0.9 copy-done
  1.5 0.0 copy-start.1
  1.5 0.9 copy-done.1
  2.4 0.0 copy-start.2
  2.4 0.9 copy-done.2
  3.3 0.0 copy-start.3
  3.3 0.9 copy-done.3
  4.3 0.0 copy-start.4
  4.3 0.8 copy-done.4
  5.0 0.0 copy-start.5
  5.0 0.7 copy-done.5
  5.7 82.9 %shard_map.93 = (bf16[128,512]{1,0:T(8,128)(2,1)S(1)}, bf16[128,512]{1,0:T(8,128)(2,1)S(1)}, bf16[128,512]{1,0:T(8,128)(2,1)S(1)}, bf16[128,512]{1,0:T(8,128)(2,1)S(1)}) custom-call(bf16[128,512]{1,0:T(8,128)(2,1)S(1)} %copy-done, bf16[128,512]{1,0:T(8,128)(2,1)S(1)} %copy-done.1, bf16[128,512]{1,0:T(8,128)(2,1)S(1)} %copy-done.2, f32[32,128]{1,0:T(8,128)S(1)} %copy-done.5, ...), custom_call_target="tpu_custom_call" | custom-call | tf_op jit(solution)/shard_map/pallas_call | solution.py:348
  88.7 0.7 copy.14
  89.3 0.7 copy.15
  90.0 0.7 copy.16
  90.6 0.7 copy.17
Async XLA Ops:
  0.6 0.9 copy-start
  1.5 0.9 copy-start.1
  2.4 0.9 copy-start.2
  3.3 0.9 copy-start.3
  4.3 0.8 copy-start.4
  5.0 0.7 copy-start.5

commit v2 on v0

v2 whole, which is shorter than its diff:
```python
import functools

import jax
import jax.numpy as jnp
from jax import lax
from jax.experimental import pallas as pl
from jax.experimental.pallas import tpu as pltpu
from jax.sharding import PartitionSpec as P

MESH = pl.DeviceIdType.MESH
BF = jnp.bfloat16
F32 = jnp.float32
SUB = 128
X_CHIPS = 4
STRIDE = 4


def broadcast_tree(size, stride):
    parent = {}
    for sgn in (1, -1):
        top = size // 2 if sgn == 1 else size // 2 - 1
        for o in range(1, top + 1):
            r = o % stride
            up = o - r + stride
            if r == 0:
                p = o - stride
            elif 2 * r > stride and up <= top:
                p = up
            else:
                p = o - r
            parent[sgn * o] = sgn * p
    kids = {}
    for o, p in parent.items():
        kids.setdefault(p, []).append(o)
    for p in kids:
        kids[p].sort(key=lambda o: -abs(o - p))
    return kids


def kernel(
    X, Z, NF,
    q_hbm, k_hbm, v_hbm, f_hbm, w_hbm, og_hbm,
    mix_o, qg_o, pg_o,
    q, k, v, filt, w, og, ext, band_f, band_b, conv, g_own, gated, stage, recv, cg, nxt, mstage, mrecv,
    load_sem, w_send, w_recv, og_send, og_recv, og_own, g_send, g_recv, g_self, r_send, r_recv,
    p_send, p_recv, c_send, c_recv, m_send, m_recv,
):
    C = X * Z
    rows, cols = w_hbm.shape
    tok, chans = q_hbm.shape
    LT = chans // SUB
    line = Z * rows
    HP = line // chans
    NG = line // SUB
    per = SUB // rows
    ctx = lax.axis_index("ctx")
    f = lax.axis_index("fsdp")
    x, z = ctx // Z, ctx % Z
    kids = broadcast_tree(Z, STRIDE)

    def dev(xx, zz, ff=None):
        return (((xx + X) % X) * Z + (zz + Z) % Z, f if ff is None else ff)

    home = f // HP == x
    barrier = pltpu.get_barrier_semaphore()
    jumps = sorted({o - p for p in kids for o in kids[p]} | {p - o for p in kids for o in kids[p]})
    partners = [dev(x, z + o) for o in jumps]
    partners += [dev(x + 1, z), dev(x - 1, z), dev(x + 2, z)]
    partners += [((ctx + 1) % C, f), ((ctx + C - 1) % C, f)]

    def hello(who):
        pl.semaphore_signal(barrier, inc=1, device_id=who, device_id_type=MESH)

    for who in partners:
        hello(who)
    for xx in range(X):
        for h in range(HP):
            ff = HP * x + h

            @pl.when(jnp.logical_or(xx != x, ff != f))
            def _():
                hello(dev(xx, z, ff))

    for ff in range(NF):
        @pl.when(jnp.logical_or(jnp.logical_not(home), ff != f))
        def _():
            hello(dev(f // HP, z, ff))

    loads = [(k_hbm, k), (v_hbm, v), (f_hbm, filt), (q_hbm, q)]
    loads = [pltpu.make_async_copy(a, b, load_sem.at[i]) for i, (a, b) in enumerate(loads)]
    mine_w = w.at[pl.ds(pl.multiple_of(z * rows, rows), rows), :]
    own_w = pltpu.make_async_copy(w_hbm, mine_w, w_recv.at[0])
    mine_og = og.at[pl.ds(pl.multiple_of(x * tok, tok), tok), :]
    own_og = pltpu.make_async_copy(og_hbm, mine_og, og_own)
    own_w.start()
    for c in loads:
        c.start()
    own_og.start()
    extra = X * HP + NF
    pl.semaphore_wait(barrier, len(partners) + jnp.where(home, extra - 2, extra))

    def remote(src, dst, ssem, rsem, who):
        pltpu.make_async_remote_copy(
            src_ref=src, dst_ref=dst, send_sem=ssem, recv_sem=rsem, device_id=who, device_id_type=MESH
        ).start()

    def wait(ref, sem):
        pltpu.make_async_copy(ref, ref, sem).wait()

    def block(zs):
        return w.at[pl.ds(pl.multiple_of((zs + Z) % Z * rows, rows), rows), :]

    def pass_on(o):
        ref = block(z - o)
        if o != 0:
            wait(ref, w_recv.at[o % Z])
        for c in kids.get(o, ()):
            remote(w_hbm if o == 0 else ref, ref, w_send, w_recv.at[c % Z], dev(x, z + c - o))

    pass_on(0)
    for s in (1, 3, 2):
        remote(og_hbm, mine_og, og_send, og_recv.at[x], dev(x + s, z))

    loads[0].wait()
    loads[1].wait()
    for j in range(LT):
        lanes = slice(j * SUB, (j + 1) * SUB)
        ext[j, tok:, :] = (k[:, lanes].astype(F32) * v[:, lanes].astype(F32)).astype(BF)

    @pl.when(ctx < C - 1)
    def _():
        remote(ext.at[:, pl.ds(tok, tok), :], ext.at[:, pl.ds(0, tok), :], p_send, p_recv, ((ctx + 1) % C, f))

    @pl.when(ctx == 0)
    def _():
        ext[:, 0:tok, :] = jnp.zeros((LT, tok, SUB), BF)

    loads[2].wait()
    taps = filt[...].astype(BF)
    i0 = lax.broadcasted_iota(jnp.int32, (SUB, 2 * SUB), 0)
    i1 = lax.broadcasted_iota(jnp.int32, (SUB, 2 * SUB), 1)

    def build(picks, band):
        base = jnp.dot(taps, jnp.where(picks, 1.0, 0.0).astype(BF), preferred_element_type=F32)
        for g in range(base.shape[0]):
            row = jnp.broadcast_to(base[g : g + 1, :], (SUB, 2 * SUB))
            band[g * SUB : (g + 1) * SUB, :] = pltpu.roll(row, 0, 1, stride=1, stride_axis=0).astype(BF)

    lane_group = lax.broadcasted_iota(jnp.int32, (tok, SUB), 1) // 16

    def apply(band, lo, hi, data, j):
        n = SUB // 16
        res = jnp.dot(band[j * n * SUB : (j + 1) * n * SUB, lo:hi], data, preferred_element_type=F32)
        out = res[0:SUB]
        for g in range(1, n):
            out = jnp.where(lane_group == g, res[g * SUB : (g + 1) * SUB], out)
        return out

    zg = z // per

    def dgate(group):
        group = (group + NG) % NG
        for i in range(per):
            zs = group * per + i
            o = (z - zs + Z) % Z

            @pl.when(o % STRIDE != 0)
            def _():
                wait(block(zs), w_recv.at[o])

        at = pl.ds(pl.multiple_of(group * SUB, SUB), SUB)
        part = lax.dot_general(
            og[...], w[at, :], (((1,), (1,)), ((), ())), preferred_element_type=F32
        ).astype(BF)
        base = x * line + group * SUB
        owner, lane = base // chans, base % chans // SUB
        for xx in range(X):
            mine = jnp.logical_and(xx == x, owner == f)
            piece = part[xx * tok : (xx + 1) * tok, :]

            @pl.when(mine)
            def _():
                recv[f, lane, :, :] = piece

            @pl.when(jnp.logical_not(mine))
            def _():
                stage[group, xx, :, :] = piece
                remote(stage.at[group, xx], recv.at[f, lane], r_send, r_recv.at[f, lane], dev(xx, z, owner))

    def dgates(first, count, step=1):
        def body(i, c):
            dgate(zg + first + i * step)
            return c

        lax.fori_loop(0, count, body, 0)

    build(i0 + i1 == SUB, band_f)
    last = Z // 2 // STRIDE
    pass_on(STRIDE)
    if last > 1:
        pass_on(-STRIDE)

    @pl.when(ctx > 0)
    def _():
        wait(ext.at[:, pl.ds(0, tok), :], p_recv)

    loads[3].wait()
    for j in range(LT):
        lanes = slice(j * SUB, (j + 1) * SUB)
        cv = apply(band_f, 0, 2 * SUB, ext[j], j)
        conv[j, :, :] = cv
        g_own[:, lanes] = (q[:, lanes].astype(F32) * cv).astype(BF)

    def gated_slot(xx, h):
        return gated.at[pl.ds(pl.multiple_of(xx * tok, tok), tok), pl.ds(pl.multiple_of(h * chans, chans), chans)]

    for s in range(NF):
        ff = (f + s) % NF

        def send_gated():
            remote(g_own, gated_slot(x, f % HP), g_send, g_recv.at[x, f % HP], dev(f // HP, z, ff))

        if s == 0:
            pl.when(jnp.logical_not(home))(send_gated)
        else:
            send_gated()

    @pl.when(home)
    def _():
        pltpu.make_async_copy(g_own, gated_slot(x, f % HP), g_self).start()

    if last > 1:
        pass_on(2 * STRIDE)
        if last > 2:
            pass_on(-2 * STRIDE)
    build(i0 == i1, band_b)
    own_w.wait()
    own_og.wait()
    for s in range(1, X):
        src = (x + s) % X
        wait(og.at[pl.ds(pl.multiple_of(src * tok, tok), tok), :], og_recv.at[src])
    done = 0
    if last > 1:
        dgates(0, 1)
        done = 1
    for m in range(3, last + 1):
        pass_on(m * STRIDE)
        if m < last:
            pass_on(-m * STRIDE)
        dgates(m - 2, 2, -2 * (m - 2))
        done += 2
    dgates(done // 2 + 1 if done else 0, NG - done)

    for xx in range(X):
        for h in range(HP):
            @pl.when(jnp.logical_or(xx != x, HP * x + h != f))
            def _():
                wait(gated_slot(xx, h), g_recv.at[xx, h])

    @pl.when(home)
    def _():
        wait(g_own, g_self)

    for s in (2, 1, 3, 0):
        xx = (x + s) % X
        part = jnp.dot(
            gated[pl.ds(pl.multiple_of(xx * tok, tok), tok), :], w[...], preferred_element_type=F32
        )
        if s == 0:
            mix_o[...] = part
        else:
            mstage[s, :, :] = part.astype(BF)
            remote(mstage.at[s], mrecv.at[x], m_send, m_recv.at[x], dev(xx, z))

    for j in range(LT):
        total = jnp.zeros((tok, SUB), F32)
        for s in range(NF):
            src = (f + s) % NF
            if s == 0:
                @pl.when(jnp.logical_not(home))
                def _():
                    wait(recv.at[src, j], r_recv.at[src, j])
            else:
                wait(recv.at[src, j], r_recv.at[src, j])
            total = total + recv[src, j, :, :].astype(F32)
        lanes = slice(j * SUB, (j + 1) * SUB)
        cg[j, :, :] = (total * q[:, lanes].astype(F32)).astype(BF)
        qg_o[:, lanes] = total * conv[j, :, :]

        @pl.when(ctx > 0)
        def _():
            remote(cg.at[j], nxt.at[j], c_send.at[j], c_recv.at[j], ((ctx + C - 1) % C, f))

    for j in range(LT):
        conv[j, :, :] = apply(band_b, 0, SUB, cg[j], j)

    mix = mix_o[...]
    for s in range(1, X):
        src = (x + s) % X
        wait(mrecv.at[src], m_recv.at[src])
        mix = mix + mrecv[src, :, :].astype(F32)
    mix_o[...] = mix

    @pl.when(ctx == C - 1)
    def _():
        nxt[...] = jnp.zeros_like(nxt)

    for j in range(LT):
        @pl.when(ctx < C - 1)
        def _():
            wait(nxt.at[j], c_recv.at[j])

        pg_o[:, j * SUB : (j + 1) * SUB] = conv[j, :, :] + apply(band_b, SUB, 2 * SUB, nxt[j], j)

    wait(w.at[pl.ds(0, (Z - 1) * rows), :], w_send)
    wait(og.at[pl.ds(0, (X - 1) * tok), :], og_send)
    wait(mrecv.at[pl.ds(0, X - 1)], m_send)
    for sem in (g_send, r_send):
        @pl.when(home)
        def _():
            wait(recv.at[pl.ds(0, NF - 1)], sem)

        @pl.when(jnp.logical_not(home))
        def _():
            wait(recv, sem)

    @pl.when(ctx < C - 1)
    def _():
        wait(ext.at[:, pl.ds(0, tok), :], p_send)

    @pl.when(ctx > 0)
    def _():
        for j in range(LT):
            wait(cg.at[j], c_send.at[j])


def solution(mesh):
    NF = mesh.shape["fsdp"]
    X = X_CHIPS
    Z = mesh.shape["ctx"] // X

    def on_device(q, k, v, f, w, og):
        tok, ch = q.shape
        lt = ch // SUB
        rows, cols = w.shape
        line = Z * rows
        dma = pltpu.SemaphoreType.DMA
        mix, qg, pg = pl.pallas_call(
            functools.partial(kernel, X, Z, NF),
            out_shape=(
                jax.ShapeDtypeStruct((tok, cols), F32),
                jax.ShapeDtypeStruct((tok, ch), F32),
                jax.ShapeDtypeStruct((tok, ch), F32),
            ),
            in_specs=[pl.BlockSpec(memory_space=pltpu.HBM)] * 6,
            out_specs=tuple([pl.BlockSpec(memory_space=pltpu.VMEM)] * 3),
            scratch_shapes=[
                pltpu.VMEM((tok, ch), BF),
                pltpu.VMEM((tok, ch), BF),
                pltpu.VMEM((tok, ch), BF),
                pltpu.VMEM(f.shape, F32),
                pltpu.VMEM((line, cols), BF),
                pltpu.VMEM((X * tok, cols), BF),
                pltpu.VMEM((lt, 2 * tok, SUB), BF),
                pltpu.VMEM((f.shape[0] * SUB, 2 * SUB), BF),
                pltpu.VMEM((f.shape[0] * SUB, 2 * SUB), BF),
                pltpu.VMEM((lt, tok, SUB), F32),
                pltpu.VMEM((tok, ch), BF),
                pltpu.VMEM((X * tok, line), BF),
                pltpu.VMEM((line // SUB, X, tok, SUB), BF),
                pltpu.VMEM((NF, lt, tok, SUB), BF),
                pltpu.VMEM((lt, tok, SUB), BF),
                pltpu.VMEM((lt, tok, SUB), BF),
                pltpu.VMEM((X, tok, cols), BF),
                pltpu.VMEM((X, tok, cols), BF),
                dma((4,)), dma, dma((Z,)), dma, dma((X,)), dma, dma, dma((X, line // ch)), dma,
                dma, dma((NF, lt)), dma, dma, dma((lt,)), dma((lt,)), dma, dma((X,)),
            ],
            compiler_params=pltpu.CompilerParams(
                collective_id=0, has_side_effects=True, vmem_limit_bytes=40 * 1024 * 1024
            ),
        )(*[pltpu.with_memory_space_constraint(a, pltpu.HBM) for a in (q, k, v, f, w, og)])
        kg = (pg * v.astype(F32)).astype(BF)
        vg = (pg * k.astype(F32)).astype(BF)
        return mix.astype(BF), qg.astype(BF), kg, vg

    wide = P("ctx", "fsdp")
    return jax.shard_map(
        on_device,
        mesh=mesh,
        in_specs=(wide, wide, wide, P("fsdp", None), wide, wide),
        out_specs=(wide, wide, wide, wide),
        check_vma=False,
    )
```

time: 508 us -> 106 us (0.21)
  waiting for transfers between devices: 325 us -> 0 us
  local copies, waits for them, and re-layouts: 137 us -> 0.34 us
  Pallas kernels: 0 us -> 103 us
  matrix products: 14.8 us -> 0 us
  between operations: 13.9 us -> 0.64 us
  starting transfers between devices: 5.4 us -> 0 us
    all_gather x2 -> x0, waiting for transfers between devices: 323 us -> none  [the longest x1 267 us: on_device(): panel_cols = lax.all_gather(out_weight, 'ctx', axis=0, tiled=True)]
    pallas_call x0 -> x1, Pallas kernels: none -> 103 us  [on_device(): pl.pallas_call(functools.partial(kernel, X, Z, NF), out_shape=(jax.ShapeD...]
    gather x3 -> x0, local copies, waits for them, and re-layouts: 81.7 us -> none  [split_band(): picked = jnp.take(filters, jnp.clip(lag_table, 0, tap_count - 1), axis=1)]
    unnamed x17 -> x4, local copies, waits for them, and re-layouts: 54.9 us -> 0.34 us
    dot_general x6 -> x0, matrix products: 14.8 us -> none  [the longest x1 4.74 us: on_device(): lax.dot_general(out_grad, panel_cols, (((1,), (1,)), ((), ())), preferred...]
    ppermute x2 -> x0, starting transfers between devices: 5.29 us -> none  [passed_along(): return lax.ppermute(block, axis, route)]
  transfers between devices with their start and end apart: 5 -> 0, of which waited for: 3 -> 0; matrix products, arithmetic and copies ran while one was open for 28% -> 0% of each run, Pallas kernels for 0% -> 0%
where the time goes in v2:
time: 106 us
  Pallas kernels  103 us (97%)
  other arithmetic  2.1 us (2%)
    pallas_call x1, Pallas kernels, on_device(): pl.pallas_call(functools.partial(kernel, X, Z, NF), out_shape=(jax.ShapeD...  103 us

profile of v2, /device:TPU:1, one launch (start us, length us, event | category | flops | bytes accessed | tf_op | source)
XLA Modules:
  0.0 105.7 jit_solution(18169290835216676687)
XLA Ops:
  0.6 102.6 %shard_map.93 = (f32[128,512]{1,0:T(8,128)S(1)}, f32[128,512]{1,0:T(8,128)S(1)}, f32[128,512]{1,0:T(8,128)S(1)}) custom-call(bf16[128,512]{1,0:T(8,128)(2,1)} %q_hbm.1, bf16[128,512]{1,0:T(8,128)(2,1)} %k_hbm.1, bf16[128,512]{1,0:T(8,128)(2,1)} %v_hbm.1, f32[32,128]{1,0:T(8,128)} %f_hbm.1, bf16[32,512]{1,0:T(8,128)(2,1)} %w_hbm.1, bf16[128,512]{1,0:T(8,128)(2,1)} %og_hbm.1), custom_call_target="tpu_custom_call" | custom-call | tf_op jit(solution)/shard_map/pallas_call | solution.py:348
  103.3 0.7 convert_element_type.18
  103.9 0.0 copy-start
  103.9 0.0 copy-start.1
  103.9 0.7 convert_element_type.19
  104.6 0.3 copy-done
  104.9 0.1 copy-done.1
  105.0 0.8 multiply_convert_fusion
Async XLA Ops:
  103.9 1.0 copy-start
  103.9 1.0 copy-start.1

commit v3 on v2

--- a/solution.py
+++ b/solution.py
@@ -41,8 +41,8 @@
     X, Z, NF,
     q_hbm, k_hbm, v_hbm, f_hbm, w_hbm, og_hbm,
     mix_o, qg_o, pg_o,
-    q, k, v, filt, w, og, ext, band_f, band_b, conv, g_own, gated, stage, recv, cg, nxt, mstage, mrecv,
-    load_sem, w_send, w_recv, og_send, og_recv, og_own, g_send, g_recv, g_self, r_send, r_recv,
+    q, k, v, filt, w, og, ext, band_f, band_b, conv, g_own, gated, gpass, stage, recv, cg, nxt, mstage, mrecv,
+    load_sem, w_send, w_recv, og_send, og_recv, og_own, g_send, gp_recv, gx_recv, gt_send, gt_recv, g_self, r_send, r_recv,
     p_send, p_recv, c_send, c_recv, m_send, m_recv,
 ):
     C = X * Z
@@ -61,12 +61,15 @@
     def dev(xx, zz, ff=None):
         return (((xx + X) % X) * Z + (zz + Z) % Z, f if ff is None else ff)
 
-    home = f // HP == x
+    y, core = f // HP, f % HP
+    twin = HP * y + (core + 1) % HP
+    home = y == x
     barrier = pltpu.get_barrier_semaphore()
     jumps = sorted({o - p for p in kids for o in kids[p]} | {p - o for p in kids for o in kids[p]})
     partners = [dev(x, z + o) for o in jumps]
     partners += [dev(x + 1, z), dev(x - 1, z), dev(x + 2, z)]
     partners += [((ctx + 1) % C, f), ((ctx + C - 1) % C, f)]
+    partners += [dev(x, z, (f + HP * t) % NF) for t in range(1, X)] + [dev(x, z, twin)]
 
     def hello(who):
         pl.semaphore_signal(barrier, inc=1, device_id=who, device_id_type=MESH)
@@ -214,26 +217,56 @@
     def gated_slot(xx, h):
         return gated.at[pl.ds(pl.multiple_of(xx * tok, tok), tok), pl.ds(pl.multiple_of(h * chans, chans), chans)]
 
-    for s in range(NF):
-        ff = (f + s) % NF
-
-        def send_gated():
-            remote(g_own, gated_slot(x, f % HP), g_send, g_recv.at[x, f % HP], dev(f // HP, z, ff))
-
-        if s == 0:
-            pl.when(jnp.logical_not(home))(send_gated)
-        else:
-            send_gated()
+    for t in (2, 1, 3):
+        who = dev(x, z, (f + HP * t) % NF)
+
+        @pl.when(home)
+        def _():
+            remote(g_own, gated_slot(x, core), g_send, gp_recv.at[y], who)
+
+        @pl.when(jnp.logical_not(home))
+        def _():
+            remote(g_own, gpass.at[y], g_send, gp_recv.at[y], who)
 
     @pl.when(home)
     def _():
-        pltpu.make_async_copy(g_own, gated_slot(x, f % HP), g_self).start()
+        pltpu.make_async_copy(g_own, gated_slot(x, core), g_self).start()
+
+    @pl.when(jnp.logical_not(home))
+    def _():
+        remote(g_own, gated_slot(x, core), g_send, gx_recv.at[x], dev(y, z))
+
+    def along_x():
+        for t in (2, 1, 3):
+            y0 = (x + t) % X
+
+            @pl.when(y0 != y)
+            def _():
+                wait(gpass.at[y0], gp_recv.at[y0])
+                remote(gpass.at[y0], gated_slot(x, core), g_send, gx_recv.at[x], dev(y0, z))
+
+    def to_twin():
+        for t in range(X):
+            x0 = (x + t) % X
+            ref = gated_slot(x0, core)
+            if t == 0:
+                @pl.when(home)
+                def _():
+                    wait(ref, g_self)
+
+                @pl.when(jnp.logical_not(home))
+                def _():
+                    wait(ref, gp_recv.at[x])
+            else:
+                wait(ref, gx_recv.at[x0])
+            remote(ref, ref, gt_send, gt_recv.at[x0], dev(x, z, twin))
 
     if last > 1:
         pass_on(2 * STRIDE)
         if last > 2:
             pass_on(-2 * STRIDE)
     build(i0 == i1, band_b)
+    along_x()
     own_w.wait()
     own_og.wait()
     for s in range(1, X):
@@ -243,23 +276,20 @@
     if last > 1:
         dgates(0, 1)
         done = 1
+    if last == 1:
+        to_twin()
     for m in range(3, last + 1):
         pass_on(m * STRIDE)
         if m < last:
             pass_on(-m * STRIDE)
         dgates(m - 2, 2, -2 * (m - 2))
+        if m == 3:
+            to_twin()
         done += 2
     dgates(done // 2 + 1 if done else 0, NG - done)
 
     for xx in range(X):
-        for h in range(HP):
-            @pl.when(jnp.logical_or(xx != x, HP * x + h != f))
-            def _():
-                wait(gated_slot(xx, h), g_recv.at[xx, h])
-
-    @pl.when(home)
-    def _():
-        wait(g_own, g_self)
+        wait(gated_slot(xx, (core + 1) % HP), gt_recv.at[xx])
 
     for s in (2, 1, 3, 0):
         xx = (x + s) % X
@@ -315,14 +345,17 @@
     wait(w.at[pl.ds(0, (Z - 1) * rows), :], w_send)
     wait(og.at[pl.ds(0, (X - 1) * tok), :], og_send)
     wait(mrecv.at[pl.ds(0, X - 1)], m_send)
-    for sem in (g_send, r_send):
-        @pl.when(home)
-        def _():
-            wait(recv.at[pl.ds(0, NF - 1)], sem)
-
-        @pl.when(jnp.logical_not(home))
-        def _():
-            wait(recv, sem)
+    wait(gpass, gt_send)
+
+    wait(recv.at[pl.ds(0, 2 * (X - 1))], g_send)
+
+    @pl.when(home)
+    def _():
+        wait(recv.at[pl.ds(0, NF - 1)], r_send)
+
+    @pl.when(jnp.logical_not(home))
+    def _():
+        wait(recv, r_send)
 
     @pl.when(ctx < C - 1)
     def _():
@@ -367,13 +400,14 @@
                 pltpu.VMEM((lt, tok, SUB), F32),
                 pltpu.VMEM((tok, ch), BF),
                 pltpu.VMEM((X * tok, line), BF),
+                pltpu.VMEM((X, tok, ch), BF),
                 pltpu.VMEM((line // SUB, X, tok, SUB), BF),
                 pltpu.VMEM((NF, lt, tok, SUB), BF),
                 pltpu.VMEM((lt, tok, SUB), BF),
                 pltpu.VMEM((lt, tok, SUB), BF),
                 pltpu.VMEM((X, tok, cols), BF),
                 pltpu.VMEM((X, tok, cols), BF),
-                dma((4,)), dma, dma((Z,)), dma, dma((X,)), dma, dma, dma((X, line // ch)), dma,
+                dma((4,)), dma, dma((Z,)), dma, dma((X,)), dma, dma, dma((X,)), dma((X,)), dma, dma((X,)), dma,
                 dma, dma((NF, lt)), dma, dma, dma((lt,)), dma((lt,)), dma, dma((X,)),
             ],
             compiler_params=pltpu.CompilerParams(

time: 106 us -> 67.1 us (0.63)
  the two profiles are of different devices: /device:TPU:1 before, /device:TPU:7 now
where the time goes in v3:
time: 67.1 us; the launch traced here: 67 us
  Pallas kernels  63.9 us (95%)
  other arithmetic  2.1 us (3%)
    pallas_call x1, Pallas kernels, on_device(): pl.pallas_call(functools.partial(kernel, X, Z, NF), out_shape=(jax.ShapeD...  63.9 us
    convert_element_type x2, other arithmetic, on_device(): return (mix.astype(BF), qg.astype(BF), kg, vg)  1.35 us

profile of v3, /device:TPU:7, one launch (start us, length us, event | category | flops | bytes accessed | tf_op | source)
XLA Modules:
  0.0 67.0 jit_solution(3384628779193596291)
XLA Ops:
  0.6 63.9 %shard_map.93 = (f32[128,512]{1,0:T(8,128)S(1)}, f32[128,512]{1,0:T(8,128)S(1)}, f32[128,512]{1,0:T(8,128)S(1)}) custom-call(bf16[128,512]{1,0:T(8,128)(2,1)} %q_hbm.1, bf16[128,512]{1,0:T(8,128)(2,1)} %k_hbm.1, bf16[128,512]{1,0:T(8,128)(2,1)} %v_hbm.1, f32[32,128]{1,0:T(8,128)} %f_hbm.1, bf16[32,512]{1,0:T(8,128)(2,1)} %w_hbm.1, bf16[128,512]{1,0:T(8,128)(2,1)} %og_hbm.1), custom_call_target="tpu_custom_call" | custom-call | tf_op jit(solution)/shard_map/pallas_call | solution.py:381
  64.5 0.7 %convert_element_type.18 = bf16[128,512]{1,0:T(8,128)(2,1)} convert(f32[128,512]{1,0:T(8,128)S(1)} %get-tuple-element.7) | non-fusion elementwise | flops 65536 | bytes 393216 | tf_op jit(solution)/shard_map/convert_element_type | solution.py:419
  65.2 0.0 copy-start
  65.2 0.0 copy-start.1
  65.2 0.7 %convert_element_type.19 = bf16[128,512]{1,0:T(8,128)(2,1)} convert(f32[128,512]{1,0:T(8,128)S(1)} %get-tuple-element.8) | non-fusion elementwise | flops 65536 | bytes 393216 | tf_op jit(solution)/shard_map/convert_element_type | solution.py:419
  65.9 0.3 copy-done
  66.2 0.1 copy-done.1
  66.2 0.8 %multiply_convert_fusion = (bf16[128,512]{1,0:T(8,128)(2,1)}, bf16[128,512]{1,0:T(8,128)(2,1)}) fusion(f32[128,512]{1,0:T(8,128)S(1)} %get-tuple-element.9, bf16[128,512]{1,0:T(8,128)(2,1)S(1)} %copy-done, bf16[128,512]{1,0:T(8,128)(2,1)S(1)} %copy-done.1), kind=kLoop, calls=%fused_computation | loop fusion | flops 393216 | bytes 786432 | tf_op jit(solution)/shard_map/convert_element_type | solution.py:418
Async XLA Ops:
  65.2 1.0 %copy-start = (bf16[128,512]{1,0:T(8,128)(2,1)S(1)}, bf16[128,512]{1,0:T(8,128)(2,1)}, u32[]{:S(2)}) copy-start(bf16[128,512]{1,0:T(8,128)(2,1)} %k_hbm.1) | copy-start | bytes 393220
  65.2 1.0 %copy-start.1 = (bf16[128,512]{1,0:T(8,128)(2,1)S(1)}, bf16[128,512]{1,0:T(8,128)(2,1)}, u32[]{:S(2)}) copy-start(bf16[128,512]{1,0:T(8,128)(2,1)} %v_hbm.1) | copy-start | bytes 393220

commit v4 on v3

--- a/solution.py
+++ b/solution.py
@@ -13,6 +13,7 @@
 SUB = 128
 X_CHIPS = 4
 STRIDE = 4
+CONV_AT, OG_AT, X_AT = 1, 2, 2
 
 
 def broadcast_tree(size, stride):
@@ -26,6 +27,8 @@
                 p = o - stride
             elif 2 * r > stride and up <= top:
                 p = up
+            elif r == 2 and stride == 4:
+                p = o - 1
             else:
                 p = o - r
             parent[sgn * o] = sgn * p
@@ -40,8 +43,8 @@
 def kernel(
     X, Z, NF,
     q_hbm, k_hbm, v_hbm, f_hbm, w_hbm, og_hbm,
-    mix_o, qg_o, pg_o,
-    q, k, v, filt, w, og, ext, band_f, band_b, conv, g_own, gated, gpass, stage, recv, cg, nxt, mstage, mrecv,
+    mix_o, qg_o, kg_o, vg_o,
+    q, k, v, filt, w, og, ext, band_f, band_b, conv, g_own, gated, gpass, mix_f, stage, recv, cg, nxt, mstage, mrecv,
     load_sem, w_send, w_recv, og_send, og_recv, og_own, g_send, gp_recv, gx_recv, gt_send, gt_recv, g_self, r_send, r_recv,
     p_send, p_recv, c_send, c_recv, m_send, m_recv,
 ):
@@ -57,6 +60,8 @@
     f = lax.axis_index("fsdp")
     x, z = ctx // Z, ctx % Z
     kids = broadcast_tree(Z, STRIDE)
+    lead = sorted((o for o in kids if o), key=lambda o: (abs(o), -o))
+    parent = {c: p for p in kids for c in kids[p]}
 
     def dev(xx, zz, ff=None):
         return (((xx + X) % X) * Z + (zz + Z) % Z, f if ff is None else ff)
@@ -153,7 +158,8 @@
 
     def apply(band, lo, hi, data, j):
         n = SUB // 16
-        res = jnp.dot(band[j * n * SUB : (j + 1) * n * SUB, lo:hi], data, preferred_element_type=F32)
+        rows_j = pl.ds(pl.multiple_of(j * n * SUB, n * SUB), n * SUB)
+        res = jnp.dot(band[rows_j, lo:hi], data, preferred_element_type=F32)
         out = res[0:SUB]
         for g in range(1, n):
             out = jnp.where(lane_group == g, res[g * SUB : (g + 1) * SUB], out)
@@ -167,7 +173,11 @@
             zs = group * per + i
             o = (z - zs + Z) % Z
 
-            @pl.when(o % STRIDE != 0)
+            leaf = o != 0
+            for ld in lead:
+                leaf = jnp.logical_and(leaf, o != ld % Z)
+
+            @pl.when(leaf)
             def _():
                 wait(block(zs), w_recv.at[o])
 
@@ -197,44 +207,8 @@
 
         lax.fori_loop(0, count, body, 0)
 
-    build(i0 + i1 == SUB, band_f)
-    last = Z // 2 // STRIDE
-    pass_on(STRIDE)
-    if last > 1:
-        pass_on(-STRIDE)
-
-    @pl.when(ctx > 0)
-    def _():
-        wait(ext.at[:, pl.ds(0, tok), :], p_recv)
-
-    loads[3].wait()
-    for j in range(LT):
-        lanes = slice(j * SUB, (j + 1) * SUB)
-        cv = apply(band_f, 0, 2 * SUB, ext[j], j)
-        conv[j, :, :] = cv
-        g_own[:, lanes] = (q[:, lanes].astype(F32) * cv).astype(BF)
-
     def gated_slot(xx, h):
         return gated.at[pl.ds(pl.multiple_of(xx * tok, tok), tok), pl.ds(pl.multiple_of(h * chans, chans), chans)]
-
-    for t in (2, 1, 3):
-        who = dev(x, z, (f + HP * t) % NF)
-
-        @pl.when(home)
-        def _():
-            remote(g_own, gated_slot(x, core), g_send, gp_recv.at[y], who)
-
-        @pl.when(jnp.logical_not(home))
-        def _():
-            remote(g_own, gpass.at[y], g_send, gp_recv.at[y], who)
-
-    @pl.when(home)
-    def _():
-        pltpu.make_async_copy(g_own, gated_slot(x, core), g_self).start()
-
-    @pl.when(jnp.logical_not(home))
-    def _():
-        remote(g_own, gated_slot(x, core), g_send, gx_recv.at[x], dev(y, z))
 
     def along_x():
         for t in (2, 1, 3):
@@ -261,32 +235,70 @@
                 wait(ref, gx_recv.at[x0])
             remote(ref, ref, gt_send, gt_recv.at[x0], dev(x, z, twin))
 
-    if last > 1:
-        pass_on(2 * STRIDE)
-        if last > 2:
-            pass_on(-2 * STRIDE)
-    build(i0 == i1, band_b)
-    along_x()
-    own_w.wait()
-    own_og.wait()
-    for s in range(1, X):
-        src = (x + s) % X
-        wait(og.at[pl.ds(pl.multiple_of(src * tok, tok), tok), :], og_recv.at[src])
-    done = 0
-    if last > 1:
-        dgates(0, 1)
-        done = 1
-    if last == 1:
-        to_twin()
-    for m in range(3, last + 1):
-        pass_on(m * STRIDE)
-        if m < last:
-            pass_on(-m * STRIDE)
-        dgates(m - 2, 2, -2 * (m - 2))
-        if m == 3:
-            to_twin()
-        done += 2
-    dgates(done // 2 + 1 if done else 0, NG - done)
+    def forward_conv():
+        @pl.when(ctx > 0)
+        def _():
+            wait(ext.at[:, pl.ds(0, tok), :], p_recv)
+
+        loads[3].wait()
+        for j in range(LT):
+            lanes = slice(j * SUB, (j + 1) * SUB)
+            cv = apply(band_f, 0, 2 * SUB, ext[j], j)
+            conv[j, :, :] = cv
+            g_own[:, lanes] = (q[:, lanes].astype(F32) * cv).astype(BF)
+        for t in (2, 1, 3):
+            who = dev(x, z, (f + HP * t) % NF)
+
+            @pl.when(home)
+            def _():
+                remote(g_own, gated_slot(x, core), g_send, gp_recv.at[y], who)
+
+            @pl.when(jnp.logical_not(home))
+            def _():
+                remote(g_own, gpass.at[y], g_send, gp_recv.at[y], who)
+
+        @pl.when(home)
+        def _():
+            pltpu.make_async_copy(g_own, gated_slot(x, core), g_self).start()
+
+        @pl.when(jnp.logical_not(home))
+        def _():
+            remote(g_own, gated_slot(x, core), g_send, gx_recv.at[x], dev(y, z))
+        build(i0 == i1, band_b)
+
+    def cotangents():
+        own_w.wait()
+        own_og.wait()
+        for s in range(1, X):
+            src = (x + s) % X
+            wait(og.at[pl.ds(pl.multiple_of(src * tok, tok), tok), :], og_recv.at[src])
+
+    build(i0 + i1 == SUB, band_f)
+    stages = Z // 2 // STRIDE
+    half = NG // 2
+    ready = 0
+    for m in range(1, stages + 1):
+        for o in lead:
+            if (m - 1) * STRIDE < abs(o) <= m * STRIDE:
+                pass_on(o)
+        if m == min(CONV_AT, stages):
+            forward_conv()
+        if m == min(OG_AT, stages):
+            cotangents()
+        if m == min(X_AT, stages):
+            along_x()
+        reach = [o for o in parent if abs(parent[o]) > (m - 1) * STRIDE]
+        reach = min(abs(o) for o in reach) if reach else Z
+        while m >= OG_AT and ready < half and per * ready + per - 1 < reach and m < stages:
+            dgates(ready, 1 if ready == 0 else 2, -2 * ready)
+            ready += 1
+    if 0 < ready < half - 1:
+        dgates(ready, 2, -2 * ready)
+        ready += 1
+    to_twin()
+    for r in range(ready, half):
+        dgates(r, 1 if r == 0 else 2, -2 * r)
+    dgates(half, 1)
 
     for xx in range(X):
         wait(gated_slot(xx, (core + 1) % HP), gt_recv.at[xx])
@@ -297,12 +309,12 @@
             gated[pl.ds(pl.multiple_of(xx * tok, tok), tok), :], w[...], preferred_element_type=F32
         )
         if s == 0:
-            mix_o[...] = part
+            mix_f[...] = part
         else:
             mstage[s, :, :] = part.astype(BF)
             remote(mstage.at[s], mrecv.at[x], m_send, m_recv.at[x], dev(xx, z))
 
-    for j in range(LT):
+    def gate_grad(j):
         total = jnp.zeros((tok, SUB), F32)
         for s in range(NF):
             src = (f + s) % NF
@@ -313,23 +325,36 @@
             else:
                 wait(recv.at[src, j], r_recv.at[src, j])
             total = total + recv[src, j, :, :].astype(F32)
-        lanes = slice(j * SUB, (j + 1) * SUB)
+        lanes = pl.ds(pl.multiple_of(j * SUB, SUB), SUB)
         cg[j, :, :] = (total * q[:, lanes].astype(F32)).astype(BF)
-        qg_o[:, lanes] = total * conv[j, :, :]
+        qg_o[:, lanes] = (total * conv[j, :, :]).astype(BF)
 
         @pl.when(ctx > 0)
         def _():
             remote(cg.at[j], nxt.at[j], c_send.at[j], c_recv.at[j], ((ctx + C - 1) % C, f))
 
+    def at_distance(dist, c):
+        def lane(j, cc):
+            ahead = (core * LT + j - zg + NG) % NG
+
+            @pl.when(jnp.minimum(ahead, (NG - ahead) % NG) == dist)
+            def _():
+                gate_grad(j)
+
+            return cc
+
+        return lax.fori_loop(0, LT, lane, c)
+
+    lax.fori_loop(0, half + 1, at_distance, 0)
     for j in range(LT):
         conv[j, :, :] = apply(band_b, 0, SUB, cg[j], j)
 
-    mix = mix_o[...]
+    mix = mix_f[...]
     for s in range(1, X):
         src = (x + s) % X
         wait(mrecv.at[src], m_recv.at[src])
         mix = mix + mrecv[src, :, :].astype(F32)
-    mix_o[...] = mix
+    mix_o[...] = mix.astype(BF)
 
     @pl.when(ctx == C - 1)
     def _():
@@ -340,7 +365,10 @@
         def _():
             wait(nxt.at[j], c_recv.at[j])
 
-        pg_o[:, j * SUB : (j + 1) * SUB] = conv[j, :, :] + apply(band_b, SUB, 2 * SUB, nxt[j], j)
+        lanes = slice(j * SUB, (j + 1) * SUB)
+        both = conv[j, :, :] + apply(band_b, SUB, 2 * SUB, nxt[j], j)
+        kg_o[:, lanes] = (both * v[:, lanes].astype(F32)).astype(BF)
+        vg_o[:, lanes] = (both * k[:, lanes].astype(F32)).astype(BF)
 
     wait(w.at[pl.ds(0, (Z - 1) * rows), :], w_send)
     wait(og.at[pl.ds(0, (X - 1) * tok), :], og_send)
@@ -365,6 +393,16 @@
     def _():
         for j in range(LT):
             wait(cg.at[j], c_send.at[j])
+
+
+def put_out(*refs):
+    sem = refs[-1]
+    n = len(refs) // 2
+    copies = [pltpu.make_async_copy(refs[i], refs[n + i], sem.at[i]) for i in range(n)]
+    for c in copies:
+        c.start()
+    for c in copies:
+        c.wait()
 
 
 def solution(mesh):
@@ -378,15 +416,11 @@
         rows, cols = w.shape
         line = Z * rows
         dma = pltpu.SemaphoreType.DMA
-        mix, qg, pg = pl.pallas_call(
+        res = pl.pallas_call(
             functools.partial(kernel, X, Z, NF),
-            out_shape=(
-                jax.ShapeDtypeStruct((tok, cols), F32),
-                jax.ShapeDtypeStruct((tok, ch), F32),
-                jax.ShapeDtypeStruct((tok, ch), F32),
-            ),
+            out_shape=[jax.ShapeDtypeStruct((tok, n), BF) for n in (cols, ch, ch, ch)],
             in_specs=[pl.BlockSpec(memory_space=pltpu.HBM)] * 6,
-            out_specs=tuple([pl.BlockSpec(memory_space=pltpu.VMEM)] * 3),
+            out_specs=[pl.BlockSpec(memory_space=pltpu.VMEM)] * 4,
             scratch_shapes=[
                 pltpu.VMEM((tok, ch), BF),
                 pltpu.VMEM((tok, ch), BF),
@@ -401,6 +435,7 @@
                 pltpu.VMEM((tok, ch), BF),
                 pltpu.VMEM((X * tok, line), BF),
                 pltpu.VMEM((X, tok, ch), BF),
+                pltpu.VMEM((tok, cols), F32),
                 pltpu.VMEM((line // SUB, X, tok, SUB), BF),
                 pltpu.VMEM((NF, lt, tok, SUB), BF),
                 pltpu.VMEM((lt, tok, SUB), BF),
@@ -414,9 +449,15 @@
                 collective_id=0, has_side_effects=True, vmem_limit_bytes=40 * 1024 * 1024
             ),
         )(*[pltpu.with_memory_space_constraint(a, pltpu.HBM) for a in (q, k, v, f, w, og)])
-        kg = (pg * v.astype(F32)).astype(BF)
-        vg = (pg * k.astype(F32)).astype(BF)
-        return mix.astype(BF), qg.astype(BF), kg, vg
+        n = len(res)
+        return pl.pallas_call(
+            put_out,
+            out_shape=[jax.ShapeDtypeStruct(r.shape, r.dtype) for r in res],
+            in_specs=[pl.BlockSpec(memory_space=pl.ANY)] * n,
+            out_specs=[pl.BlockSpec(memory_space=pl.ANY)] * n,
+            scratch_shapes=[dma((n,))],
+            compiler_params=pltpu.CompilerParams(vmem_limit_bytes=1024 * 1024),
+        )(*res)
 
     wide = P("ctx", "fsdp")
     return jax.shard_map(

time: 67.1 us -> 65.3 us (0.973)
  the two profiles are of different devices: /device:TPU:7 before, /device:TPU:1 now
where the time goes in v4:
time: 65.3 us; the launch traced here: 64.9 us
  Pallas kernels  64.3 us (98%)
    pallas_call x1, Pallas kernels, on_device(): pl.pallas_call(functools.partial(kernel, X, Z, NF), out_shape=[jax.ShapeD...  63.4 us

profile of v4, /device:TPU:1, one launch (start us, length us, event | category | flops | bytes accessed | tf_op | source)
XLA Modules:
  0.0 64.9 jit_solution(8525968401183773012)
XLA Ops:
  0.6 63.4 %shard_map.93 = (bf16[128,512]{1,0:T(8,128)(2,1)S(1)}, bf16[128,512]{1,0:T(8,128)(2,1)S(1)}, bf16[128,512]{1,0:T(8,128)(2,1)S(1)}, bf16[128,512]{1,0:T(8,128)(2,1)S(1)}) custom-call(bf16[128,512]{1,0:T(8,128)(2,1)} %q_hbm.1, bf16[128,512]{1,0:T(8,128)(2,1)} %k_hbm.1, bf16[128,512]{1,0:T(8,128)(2,1)} %v_hbm.1, f32[32,128]{1,0:T(8,128)} %f_hbm.1, ...), custom_call_target="tpu_custom_call" | custom-call | tf_op jit(solution)/shard_map/pallas_call | solution.py:419
  64.1 0.8 %shard_map.94 = (bf16[128,512]{1,0:T(8,128)(2,1)}, bf16[128,512]{1,0:T(8,128)(2,1)}, bf16[128,512]{1,0:T(8,128)(2,1)}, bf16[128,512]{1,0:T(8,128)(2,1)}) custom-call(bf16[128,512]{1,0:T(8,128)(2,1)S(1)} %get-tuple-element.8.refs_0_, bf16[128,512]{1,0:T(8,128)(2,1)S(1)} %get-tuple-element.9.refs_1_, bf16[128,512]{1,0:T(8,128)(2,1)S(1)} %get-tuple-element.10.refs_2_, ...), custom_call_target="tpu_custom_call" | custom-call | tf_op jit(solution)/shard_map/pallas_call | solution.py:453

commit v5 on v4

--- a/solution.py
+++ b/solution.py
@@ -280,6 +280,9 @@
     for m in range(1, stages + 1):
         for o in lead:
             if (m - 1) * STRIDE < abs(o) <= m * STRIDE:
+                if o == Z // 2 and 0 < ready < half - 1:
+                    dgates(ready, 2, -2 * ready)
+                    ready += 1
                 pass_on(o)
         if m == min(CONV_AT, stages):
             forward_conv()
@@ -292,13 +295,10 @@
         while m >= OG_AT and ready < half and per * ready + per - 1 < reach and m < stages:
             dgates(ready, 1 if ready == 0 else 2, -2 * ready)
             ready += 1
-    if 0 < ready < half - 1:
-        dgates(ready, 2, -2 * ready)
-        ready += 1
-    to_twin()
     for r in range(ready, half):
         dgates(r, 1 if r == 0 else 2, -2 * r)
     dgates(half, 1)
+    to_twin()
 
     for xx in range(X):
         wait(gated_slot(xx, (core + 1) % HP), gt_recv.at[xx])
@@ -349,26 +349,26 @@
     for j in range(LT):
         conv[j, :, :] = apply(band_b, 0, SUB, cg[j], j)
 
+    @pl.when(ctx == C - 1)
+    def _():
+        nxt[...] = jnp.zeros_like(nxt)
+
+    for j in range(LT):
+        @pl.when(ctx < C - 1)
+        def _():
+            wait(nxt.at[j], c_recv.at[j])
+
+        lanes = slice(j * SUB, (j + 1) * SUB)
+        both = conv[j, :, :] + apply(band_b, SUB, 2 * SUB, nxt[j], j)
+        kg_o[:, lanes] = (both * v[:, lanes].astype(F32)).astype(BF)
+        vg_o[:, lanes] = (both * k[:, lanes].astype(F32)).astype(BF)
+
     mix = mix_f[...]
     for s in range(1, X):
         src = (x + s) % X
         wait(mrecv.at[src], m_recv.at[src])
         mix = mix + mrecv[src, :, :].astype(F32)
     mix_o[...] = mix.astype(BF)
-
-    @pl.when(ctx == C - 1)
-    def _():
-        nxt[...] = jnp.zeros_like(nxt)
-
-    for j in range(LT):
-        @pl.when(ctx < C - 1)
-        def _():
-            wait(nxt.at[j], c_recv.at[j])
-
-        lanes = slice(j * SUB, (j + 1) * SUB)
-        both = conv[j, :, :] + apply(band_b, SUB, 2 * SUB, nxt[j], j)
-        kg_o[:, lanes] = (both * v[:, lanes].astype(F32)).astype(BF)
-        vg_o[:, lanes] = (both * k[:, lanes].astype(F32)).astype(BF)
 
     wait(w.at[pl.ds(0, (Z - 1) * rows), :], w_send)
     wait(og.at[pl.ds(0, (X - 1) * tok), :], og_send)

time: 65.3 us -> 64.2 us (0.983)
  Pallas kernels: 64.3 us -> 63.2 us
    pallas_call x1, Pallas kernels: 63.4 us -> 62.4 us  [on_device(): pl.pallas_call(functools.partial(kernel, X, Z, NF), out_shape=[jax.ShapeD...]
where the time goes in v5:
time: 64.2 us; the launch traced here: 63.8 us
  Pallas kernels  63.2 us (98%)
    pallas_call x1, Pallas kernels, on_device(): pl.pallas_call(functools.partial(kernel, X, Z, NF), out_shape=[jax.ShapeD...  62.4 us

profile of v5, /device:TPU:1, one launch (start us, length us, event | category | flops | bytes accessed | tf_op | source)
XLA Modules:
  0.0 63.8 jit_solution(6185858916717085694)
XLA Ops:
  0.6 62.4 %shard_map.93 = (bf16[128,512]{1,0:T(8,128)(2,1)S(1)}, bf16[128,512]{1,0:T(8,128)(2,1)S(1)}, bf16[128,512]{1,0:T(8,128)(2,1)S(1)}, bf16[128,512]{1,0:T(8,128)(2,1)S(1)}) custom-call(bf16[128,512]{1,0:T(8,128)(2,1)} %q_hbm.1, bf16[128,512]{1,0:T(8,128)(2,1)} %k_hbm.1, bf16[128,512]{1,0:T(8,128)(2,1)} %v_hbm.1, f32[32,128]{1,0:T(8,128)} %f_hbm.1, ...), custom_call_target="tpu_custom_call" | custom-call | tf_op jit(solution)/shard_map/pallas_call | solution.py:419
  63.0 0.8 %shard_map.94 = (bf16[128,512]{1,0:T(8,128)(2,1)}, bf16[128,512]{1,0:T(8,128)(2,1)}, bf16[128,512]{1,0:T(8,128)(2,1)}, bf16[128,512]{1,0:T(8,128)(2,1)}) custom-call(bf16[128,512]{1,0:T(8,128)(2,1)S(1)} %get-tuple-element.8.refs_0_, bf16[128,512]{1,0:T(8,128)(2,1)S(1)} %get-tuple-element.9.refs_1_, bf16[128,512]{1,0:T(8,128)(2,1)S(1)} %get-tuple-element.10.refs_2_, ...), custom_call_target="tpu_custom_call" | custom-call | tf_op jit(solution)/shard_map/pallas_call | solution.py:453

commit v6 on v5

--- a/solution.py
+++ b/solution.py
@@ -188,17 +188,18 @@
         base = x * line + group * SUB
         owner, lane = base // chans, base % chans // SUB
         for xx in range(X):
-            mine = jnp.logical_and(xx == x, owner == f)
-            piece = part[xx * tok : (xx + 1) * tok, :]
-
-            @pl.when(mine)
-            def _():
-                recv[f, lane, :, :] = piece
-
-            @pl.when(jnp.logical_not(mine))
-            def _():
-                stage[group, xx, :, :] = piece
-                remote(stage.at[group, xx], recv.at[f, lane], r_send, r_recv.at[f, lane], dev(xx, z, owner))
+            stage[group, xx, :, :] = part[xx * tok : (xx + 1) * tok, :]
+        for s in (2, 1, 3):
+            xx = (x + s) % X
+            remote(stage.at[group, xx], recv.at[f, lane], r_send, r_recv.at[f, lane], dev(xx, z, owner))
+
+        @pl.when(owner == f)
+        def _():
+            recv[f, lane, :, :] = stage[group, x, :, :]
+
+        @pl.when(owner != f)
+        def _():
+            remote(stage.at[group, x], recv.at[f, lane], r_send, r_recv.at[f, lane], dev(x, z, owner))
 
     def dgates(first, count, step=1):
         def body(i, c):

time: 64.2 us -> 64.2 us (level)
  no operation moved by 1% of the time
where the time goes in v6:
time: 64.2 us; the launch traced here: 63.8 us
  Pallas kernels  63.2 us (98%)
    pallas_call x1, Pallas kernels, on_device(): pl.pallas_call(functools.partial(kernel, X, Z, NF), out_shape=[jax.ShapeD...  62.3 us

profile of v6, /device:TPU:1, one launch (start us, length us, event | category | flops | bytes accessed | tf_op | source)
XLA Modules:
  0.0 63.8 jit_solution(2131801433314915568)
XLA Ops:
  0.6 62.3 %shard_map.93 = (bf16[128,512]{1,0:T(8,128)(2,1)S(1)}, bf16[128,512]{1,0:T(8,128)(2,1)S(1)}, bf16[128,512]{1,0:T(8,128)(2,1)S(1)}, bf16[128,512]{1,0:T(8,128)(2,1)S(1)}) custom-call(bf16[128,512]{1,0:T(8,128)(2,1)} %q_hbm.1, bf16[128,512]{1,0:T(8,128)(2,1)} %k_hbm.1, bf16[128,512]{1,0:T(8,128)(2,1)} %v_hbm.1, f32[32,128]{1,0:T(8,128)} %f_hbm.1, ...), custom_call_target="tpu_custom_call" | custom-call | tf_op jit(solution)/shard_map/pallas_call | solution.py:420
  63.0 0.8 %shard_map.94 = (bf16[128,512]{1,0:T(8,128)(2,1)}, bf16[128,512]{1,0:T(8,128)(2,1)}, bf16[128,512]{1,0:T(8,128)(2,1)}, bf16[128,512]{1,0:T(8,128)(2,1)}) custom-call(bf16[128,512]{1,0:T(8,128)(2,1)S(1)} %get-tuple-element.8.refs_0_, bf16[128,512]{1,0:T(8,128)(2,1)S(1)} %get-tuple-element.9.refs_1_, bf16[128,512]{1,0:T(8,128)(2,1)S(1)} %get-tuple-element.10.refs_2_, ...), custom_call_target="tpu_custom_call" | custom-call | tf_op jit(solution)/shard_map/pallas_call | solution.py:454
